TPU v7x, 32 devices: a whole 2x2x4 slice. The times are simulated.
32 devices in a mesh: pair: 16 (over z, y, core), split: 2 (over x).
Axes of the slice: x: 2, y: 2, z: 4, core: 2. Of those that a mesh axis runs over, the one named last changes fastest.
Arguments:
- descriptors: bfloat16 [16, 1024, 256], P('pair', 'split'), as said below
- points: bfloat16 [16, 3, 1024], P('pair', None, 'split'), may hold values from -6 to 6
- normals: bfloat16 [16, 3, 1024], P('pair', None, 'split'), may hold values from -6 to 6
- pair_list: int32 [384, 2], replicated, may hold values from 0 to 15, as said below
- intersection: int32 [384], P('pair'), may hold values from 256 to 1024
- pose_index: int32 [16], replicated, may hold values from 0 to 15, each once
Outputs:
- pair_cross: float32 [384, 6, 6], P('pair')
- pose_hessian: float32 [16, 6, 6], P('pair')
- pose_gradient: float32 [16, 6], P('pair')
Inputs may be any that keep to these rules, and one draw needn't show every extreme that they name: `descriptors`: values stay within -24 to 24. `pair_list`: task k's source scan is scan k // 24. The owner of a scan s is s; a task's target has another owner than its source. Among the 24 tasks of one aligned block (tasks k // 24 alike), no owner holds the targets of more than 2 of them, and some owner holds exactly 2.
All inputs are finite; a program needn't handle non-finite values.
Results may differ from a plain program's by a relative error of at most 0.0003.
Values may be sent and summed in bfloat16 or wider, within the bound.
A program may use at most 64 MiB of HBM per device.

v0:
```python
import jax
import jax.numpy as jnp
from jax import lax
from jax.sharding import PartitionSpec as P

task_group = 4


def merged(shard, axis, combine):
    everything = jax.tree.map(lambda part: lax.all_gather(part, axis), shard)
    leading = jax.tree.map(lambda part: part[0], everything)

    def hop(k, so_far):
        return combine(so_far, jax.tree.map(lambda part: part[k], everything))

    return lax.fori_loop(1, lax.axis_size(axis), hop, leading)


def cross_second(left_vec, right_vec):
    return jnp.stack(
        [
            left_vec[:, 1] * right_vec[:, 2] - left_vec[:, 2] * right_vec[:, 1],
            left_vec[:, 2] * right_vec[:, 0] - left_vec[:, 0] * right_vec[:, 2],
            left_vec[:, 0] * right_vec[:, 1] - left_vec[:, 1] * right_vec[:, 0],
        ],
        axis=1,
    )


def assemble(softened, source, row_seen, counts, all_rows):
    highest = lax.Precision.HIGHEST
    matched = softened[:, :3]
    normal = softened[:, 3:]
    weight = (row_seen[None, :] < counts[:, None]).astype(jnp.float32)
    jacobian = jnp.concatenate(
        [cross_second(source, normal), normal, -cross_second(matched, normal), -normal], axis=1
    )
    residual = jnp.sum(normal * (source - matched), axis=1)
    weighted = jacobian * weight[:, None, :]
    hessian = jnp.einsum("tan,tbn->tab", weighted, jacobian, precision=highest) / all_rows
    gradient = jnp.einsum("tan,tn->ta", weighted, residual, precision=highest) / all_rows
    return (hessian, gradient)


def unite(earlier, later):
    highest_score = jnp.maximum(earlier[0], later[0])
    factor_early = jnp.exp(earlier[0] - highest_score)
    factor_late = jnp.exp(later[0] - highest_score)
    return (
        highest_score,
        earlier[1] * factor_early + later[1] * factor_late,
        earlier[2] * factor_early[:, None, :] + later[2] * factor_late[:, None, :],
    )


def per_device(descriptors, points, normals, pair_list, intersection, pose_index):
    highest = lax.Precision.HIGHEST
    scan_dev, block_rows, feature_width = descriptors.shape
    split_count = lax.axis_size("split")
    own_index = lax.axis_index("pair")
    all_rows = block_rows * split_count
    task_count = intersection.shape[0]
    my_pairs = lax.dynamic_slice_in_dim(pair_list, own_index * task_count, task_count, 0)
    sources = my_pairs[:, 0] - own_index * scan_dev
    targets = my_pairs[:, 1]
    geometry = jnp.concatenate([points, normals], axis=1)
    source_desc, source_points = (
        lax.all_gather(descriptors, "split", axis=1, tiled=True),
        lax.all_gather(points, "split", axis=2, tiled=True),
    )
    target_desc, target_geometry = (
        lax.all_gather(descriptors, "pair", axis=0, tiled=True),
        lax.all_gather(geometry, "pair", axis=0, tiled=True),
    )
    score_scale = feature_width ** (-0.5)
    group_count = task_count // task_group

    def attend(indices):
        source_ids, tile_ids = indices
        queries = source_desc[source_ids]
        key_rows = target_desc[tile_ids]
        tile_geometry = target_geometry[tile_ids].astype(jnp.float32)
        scores = (
            jnp.einsum("gic,gjc->gij", queries, key_rows, preferred_element_type=jnp.float32)
            * score_scale
        )
        maxima = jnp.max(scores, axis=2)
        exponent = jnp.exp(scores - maxima[:, :, None])
        totals = jnp.sum(exponent, axis=2)
        moment = jnp.einsum("gij,gdj->gdi", exponent, tile_geometry, precision=highest)
        return (maxima, totals, moment)

    maxima, totals, moment = lax.map(
        attend, (sources.reshape(group_count, task_group), targets.reshape(group_count, task_group))
    )
    maxima = maxima.reshape(task_count, all_rows)
    totals = totals.reshape(task_count, all_rows)
    moment = moment.reshape(task_count, 6, all_rows)
    maxima, totals, moment = merged((maxima, totals, moment), "split", unite)
    softened = moment / totals[:, None, :]
    row_seen = jnp.arange(all_rows, dtype=jnp.int32)
    hessian, gradient = assemble(
        softened, source_points[sources].astype(jnp.float32), row_seen, intersection, all_rows
    )
    pair_cross = hessian[:, :6, 6:]
    all_poses = pose_index.shape[0]
    source_pose = pose_index[my_pairs[:, 0]]
    target_pose = pose_index[targets]
    source_part = jnp.concatenate(
        [hessian[:, :6, :6].reshape(task_count, 36), gradient[:, :6]], axis=1
    )
    target_part = jnp.concatenate(
        [hessian[:, 6:, 6:].reshape(task_count, 36), gradient[:, 6:]], axis=1
    )
    pose_slots = jnp.arange(all_poses, dtype=jnp.int32)[:, None]
    onehot_source = (pose_slots == source_pose[None, :]).astype(jnp.float32)
    onehot_target = (pose_slots == target_pose[None, :]).astype(jnp.float32)
    pose_terms = (
        jnp.dot(onehot_source, source_part, precision=highest)
        + jnp.dot(onehot_target, target_part, precision=highest)
    ) / task_count
    hessian_rows, gradient_rows = (
        lax.psum_scatter(pose_terms[:, :36], "pair", scatter_dimension=0, tiled=True),
        lax.psum_scatter(pose_terms[:, 36:], "pair", scatter_dimension=0, tiled=True),
    )
    return (pair_cross, hessian_rows.reshape(-1, 6, 6), gradient_rows)


def solution(mesh):
    in_specs = (
        P("pair", "split", None),
        P("pair", None, "split"),
        P("pair", None, "split"),
        P(),
        P("pair"),
        P(),
    )
    out_specs = (P("pair", None, None), P("pair", None, None), P("pair", None))
    return jax.shard_map(
        per_device, mesh=mesh, in_specs=in_specs, out_specs=out_specs, check_vma=False
    )
```

profile of v0, /device:TPU:0, one launch (start us, length us, event | category | flops | bytes accessed | tf_op | source)
XLA Modules:
  0.0 269.5 jit_solution(10268699834925896939)
XLA Ops:
  8.9 23.6 %all_gather.24 = bf16[16,6,512]{2,1,0:T(8,128)(2,1)S(1)} all-gather(bf16[1,6,512]{2,1,0:T(8,128)(2,1)S(1)} %pad_maximum_fusion), channel_id=1, replica_groups=mesh['pair'=16,'split'=2] {'pair'}, dimensions={0}, use_global_device_ids=true | all-gather | bytes 104448 | tf_op jit(solution)/shard_map/all_gather | solution.py:73
  32.5 9.4 %all_gather.22 = bf16[1,1024,256]{2,1,0:T(8,128)(2,1)S(1)} all-gather(bf16[1,512,256]{2,1,0:T(8,128)(2,1)} %param.8), channel_id=1, replica_groups=mesh['pair'=16,'split'=2] {'split'}, dimensions={1}, use_global_device_ids=true | all-gather | bytes 786432 | tf_op jit(solution)/shard_map/all_gather | solution.py:68
  41.9 21.4 %all-gather.3.cloned.1.call-done = bf16[16,512,256]{2,1,0:T(8,128)(2,1)} async-done(((bf16[1,512,256]{2,1,0:T(8,128)(2,1)}), bf16[16,512,256]{2,1,0:T(8,128)(2,1)}) %all-gather.3.cloned.1.call-update) | async-done | bytes 4194320 | tf_op jit(solution)/shard_map/all_gather | solution.py:72
  63.3 100.4 %while.3 = (s32[]{:T(128)}, f32[6,4,1024]{2,1,0:T(4,128)S(1)}, f32[6,4,1024]{2,1,0:T(4,128)S(1)}, f32[6,4,6,1024]{3,2,1,0:T(8,128)S(1)}, bf16[1,1024,256]{2,1,0:...) while((s32[]{:T(128)}, f32[6,4,1024]{2,1,0:T(4,128)S(1)}, ...), condition=%wide.region_3.4_spmd.clone, body=%wide.region_0.3_spmd.clone.sunk | while | flops 1239409664 | bytes 62738644 | solution.py:93
  66.1 4.5 %bitcast_reduce_fusion.2 = (f32[4,1024]{1,0:T(4,128)S(1)}, f32[4,512,1024]{2,1,0:T(8,128)}) fusion(bf16[4,512,256]{2,1,0:T(8,128)(2,1)S(1)} %gather_fusion, bf16[1024,256]{1,0:T(8,128)(2,1)S(1)} %bitcast.108), kind=kOutput, calls=%fused_computation.5.clone.1 | convolution fusion | flops 1077932032 | bytes 9977856 | tf_op jit(solution)/shard_map/while/body/eval_jaxpr/gic,gjc->gij/dot_general | solution.py:84
  71.2 7.4 %fusion.74 = f32[6,4,6,1024]{3,2,1,0:T(8,128)S(1)} fusion(f32[6,4,6,1024]{3,2,1,0:T(8,128)S(1)} %get-tuple-element.222, s32[]{:T(128)} %get-tuple-element.219, bf16[4,6,512]{2,1,0:T(8,128)(2,1)S(1)} %gather_fusion.1, f32[4,512,1024]{2,1,0:T(8,128)} %get-tuple-element.206, f32[4,1024]{1,0:T(4,128)S(1)} %get-tuple-element.207), kind=kOutput, calls=%fused_computation.12.clone.1 | convolution fusion | flops 155189248 | bytes 8568836 | tf_op jit(solution)/shard_map/while/body/eval_jaxpr/gij,gdj->gdi/dot_general | solution.py:90
  80.1 2.8 %gather_fusion = bf16[4,512,256]{2,1,0:T(8,128)(2,1)S(1)} fusion(bf16[16,512,256]{2,1,0:T(8,128)(2,1)} %get-tuple-element.234, s32[1024]{0:T(1024)S(1)} %pad_clamp_fusion.4), kind=kCustom, calls=%fused_computation.clone.1 | custom fusion | bytes 2097168 | tf_op jit(solution)/shard_map/while/body/eval_jaxpr/gather | solution.py:81
  82.9 4.5 %bitcast_reduce_fusion.2 = (f32[4,1024]{1,0:T(4,128)S(1)}, f32[4,512,1024]{2,1,0:T(8,128)}) fusion(bf16[4,512,256]{2,1,0:T(8,128)(2,1)S(1)} %gather_fusion, bf16[1024,256]{1,0:T(8,128)(2,1)S(1)} %bitcast.108), kind=kOutput, calls=%fused_computation.5.clone.1 | convolution fusion | flops 1077932032 | bytes 9977856 | tf_op jit(solution)/shard_map/while/body/eval_jaxpr/gic,gjc->gij/dot_general | solution.py:84
  88.0 7.4 %fusion.74 = f32[6,4,6,1024]{3,2,1,0:T(8,128)S(1)} fusion(f32[6,4,6,1024]{3,2,1,0:T(8,128)S(1)} %get-tuple-element.222, s32[]{:T(128)} %get-tuple-element.219, bf16[4,6,512]{2,1,0:T(8,128)(2,1)S(1)} %gather_fusion.1, f32[4,512,1024]{2,1,0:T(8,128)} %get-tuple-element.206, f32[4,1024]{1,0:T(4,128)S(1)} %get-tuple-element.207), kind=kOutput, calls=%fused_computation.12.clone.1 | convolution fusion | flops 155189248 | bytes 8568836 | tf_op jit(solution)/shard_map/while/body/eval_jaxpr/gij,gdj->gdi/dot_general | solution.py:90
  96.8 2.8 %gather_fusion = bf16[4,512,256]{2,1,0:T(8,128)(2,1)S(1)} fusion(bf16[16,512,256]{2,1,0:T(8,128)(2,1)} %get-tuple-element.234, s32[1024]{0:T(1024)S(1)} %pad_clamp_fusion.4), kind=kCustom, calls=%fused_computation.clone.1 | custom fusion | bytes 2097168 | tf_op jit(solution)/shard_map/while/body/eval_jaxpr/gather | solution.py:81
  99.6 4.5 %bitcast_reduce_fusion.2 = (f32[4,1024]{1,0:T(4,128)S(1)}, f32[4,512,1024]{2,1,0:T(8,128)}) fusion(bf16[4,512,256]{2,1,0:T(8,128)(2,1)S(1)} %gather_fusion, bf16[1024,256]{1,0:T(8,128)(2,1)S(1)} %bitcast.108), kind=kOutput, calls=%fused_computation.5.clone.1 | convolution fusion | flops 1077932032 | bytes 9977856 | tf_op jit(solution)/shard_map/while/body/eval_jaxpr/gic,gjc->gij/dot_general | solution.py:84
  104.7 7.4 %fusion.74 = f32[6,4,6,1024]{3,2,1,0:T(8,128)S(1)} fusion(f32[6,4,6,1024]{3,2,1,0:T(8,128)S(1)} %get-tuple-element.222, s32[]{:T(128)} %get-tuple-element.219, bf16[4,6,512]{2,1,0:T(8,128)(2,1)S(1)} %gather_fusion.1, f32[4,512,1024]{2,1,0:T(8,128)} %get-tuple-element.206, f32[4,1024]{1,0:T(4,128)S(1)} %get-tuple-element.207), kind=kOutput, calls=%fused_computation.12.clone.1 | convolution fusion | flops 155189248 | bytes 8568836 | tf_op jit(solution)/shard_map/while/body/eval_jaxpr/gij,gdj->gdi/dot_general | solution.py:90
  116.4 4.5 %bitcast_reduce_fusion.2 = (f32[4,1024]{1,0:T(4,128)S(1)}, f32[4,512,1024]{2,1,0:T(8,128)}) fusion(bf16[4,512,256]{2,1,0:T(8,128)(2,1)S(1)} %gather_fusion, bf16[1024,256]{1,0:T(8,128)(2,1)S(1)} %bitcast.108), kind=kOutput, calls=%fused_computation.5.clone.1 | convolution fusion | flops 1077932032 | bytes 9977856 | tf_op jit(solution)/shard_map/while/body/eval_jaxpr/gic,gjc->gij/dot_general | solution.py:84
  121.5 7.4 %fusion.74 = f32[6,4,6,1024]{3,2,1,0:T(8,128)S(1)} fusion(f32[6,4,6,1024]{3,2,1,0:T(8,128)S(1)} %get-tuple-element.222, s32[]{:T(128)} %get-tuple-element.219, bf16[4,6,512]{2,1,0:T(8,128)(2,1)S(1)} %gather_fusion.1, f32[4,512,1024]{2,1,0:T(8,128)} %get-tuple-element.206, f32[4,1024]{1,0:T(4,128)S(1)} %get-tuple-element.207), kind=kOutput, calls=%fused_computation.12.clone.1 | convolution fusion | flops 155189248 | bytes 8568836 | tf_op jit(solution)/shard_map/while/body/eval_jaxpr/gij,gdj->gdi/dot_general | solution.py:90
  133.1 4.5 %bitcast_reduce_fusion.2 = (f32[4,1024]{1,0:T(4,128)S(1)}, f32[4,512,1024]{2,1,0:T(8,128)}) fusion(bf16[4,512,256]{2,1,0:T(8,128)(2,1)S(1)} %gather_fusion, bf16[1024,256]{1,0:T(8,128)(2,1)S(1)} %bitcast.108), kind=kOutput, calls=%fused_computation.5.clone.1 | convolution fusion | flops 1077932032 | bytes 9977856 | tf_op jit(solution)/shard_map/while/body/eval_jaxpr/gic,gjc->gij/dot_general | solution.py:84
  138.2 7.4 %fusion.74 = f32[6,4,6,1024]{3,2,1,0:T(8,128)S(1)} fusion(f32[6,4,6,1024]{3,2,1,0:T(8,128)S(1)} %get-tuple-element.222, s32[]{:T(128)} %get-tuple-element.219, bf16[4,6,512]{2,1,0:T(8,128)(2,1)S(1)} %gather_fusion.1, f32[4,512,1024]{2,1,0:T(8,128)} %get-tuple-element.206, f32[4,1024]{1,0:T(4,128)S(1)} %get-tuple-element.207), kind=kOutput, calls=%fused_computation.12.clone.1 | convolution fusion | flops 155189248 | bytes 8568836 | tf_op jit(solution)/shard_map/while/body/eval_jaxpr/gij,gdj->gdi/dot_general | solution.py:90
  149.9 4.5 %bitcast_reduce_fusion.2 = (f32[4,1024]{1,0:T(4,128)S(1)}, f32[4,512,1024]{2,1,0:T(8,128)}) fusion(bf16[4,512,256]{2,1,0:T(8,128)(2,1)S(1)} %gather_fusion, bf16[1024,256]{1,0:T(8,128)(2,1)S(1)} %bitcast.108), kind=kOutput, calls=%fused_computation.5.clone.1 | convolution fusion | flops 1077932032 | bytes 9977856 | tf_op jit(solution)/shard_map/while/body/eval_jaxpr/gic,gjc->gij/dot_general | solution.py:84
  154.9 7.4 %fusion.74 = f32[6,4,6,1024]{3,2,1,0:T(8,128)S(1)} fusion(f32[6,4,6,1024]{3,2,1,0:T(8,128)S(1)} %get-tuple-element.222, s32[]{:T(128)} %get-tuple-element.219, bf16[4,6,512]{2,1,0:T(8,128)(2,1)S(1)} %gather_fusion.1, f32[4,512,1024]{2,1,0:T(8,128)} %get-tuple-element.206, f32[4,1024]{1,0:T(4,128)S(1)} %get-tuple-element.207), kind=kOutput, calls=%fused_computation.12.clone.1 | convolution fusion | flops 155189248 | bytes 8568836 | tf_op jit(solution)/shard_map/while/body/eval_jaxpr/gij,gdj->gdi/dot_general | solution.py:90
  167.0 4.3 %all_gather.21 = bf16[1,3,1024]{2,1,0:T(4,128)(2,1)S(1)} all-gather(bf16[1,3,512]{2,1,0:T(4,128)(2,1)S(1)} %copy-done.3), channel_id=1, replica_groups=mesh['pair'=16,'split'=2] {'split'}, dimensions={2}, use_global_device_ids=true | all-gather | bytes 9216 | tf_op jit(solution)/shard_map/all_gather | solution.py:69
  171.6 7.8 %all_gather.26 = f32[2,24,1024]{2,1,0:T(8,128)S(1)} all-gather(f32[1,24,1024]{2,1,0:T(8,128)S(1)} %all_gather_reshape.10), channel_id=1, replica_groups=mesh['pair'=16,'split'=2] {'split'}, dimensions={0}, use_global_device_ids=true | all-gather | bytes 294912 | tf_op jit(solution)/shard_map/all_gather | solution.py:10
  179.3 7.7 %all_gather.27 = f32[2,24,1024]{2,1,0:T(8,128)S(1)} all-gather(f32[1,24,1024]{2,1,0:T(8,128)S(1)} %all_gather_reshape.11), channel_id=1, replica_groups=mesh['pair'=16,'split'=2] {'split'}, dimensions={0}, use_global_device_ids=true | all-gather | bytes 294912 | tf_op jit(solution)/shard_map/all_gather | solution.py:10
  187.1 3.5 %all-gather.5.cloned.1.call-done = f32[2,24,6,1024]{3,1,2,0:T(8,128)} async-done(((f32[1,24,6,1024]{3,1,2,0:T(8,128)}), f32[2,24,6,1024]{3,1,2,0:T(8,128)}) %all-gather.5.cloned.1.call-update) | async-done | bytes 1179664 | tf_op jit(solution)/shard_map/all_gather | solution.py:10
  192.4 3.5 %fusion.22 = f32[24,12,12]{2,1,0:T(8,128)S(1)} fusion(f32[24,12,1024]{2,0,1:T(8,128)S(1)} %negate_dynamic-update-slice_fusion, f32[24,12,1024]{2,0,1:T(8,128)S(1)} %broadcast_multiply_fusion), kind=kOutput, calls=%fused_computation.28 | convolution fusion | flops 42470784 | bytes 2373120 | tf_op jit(solution)/shard_map/tan,tbn->tab/dot_general | solution.py:40
  199.4 60.1 %all-reduce.2 = (f32[16,36]{1,0:T(8,128)S(1)}, f32[16,6]{1,0:T(8,128)S(1)}) all-reduce(f32[16,36]{1,0:T(8,128)S(1)} %bitcast.111, f32[16,6]{1,0:T(8,128)S(1)} %slice.151), channel_id=2, replica_groups=mesh['pair'=16,'split'=2] {'pair'}, use_global_device_ids=true, to_apply=%region_5.6.clone | all-reduce | flops 672 | bytes 5376
  (102 shorter events, 36.6 us)
Async XLA Ops:
  7.2 0.8 copy-start
  7.2 56.1 %all-gather.3.cloned.1.call-start = ((), (), s32[]{:S(2)}) async-start(), calls=%async_computation | async-start | bytes 4456448 | tf_op jit(solution)/shard_map/all_gather | solution.py:72
  7.9 182.7 %all-gather.5.cloned.1.call-start = ((), (), s32[]{:S(2)}) async-start(), calls=%async_computation.1 | async-start | bytes 1769472 | tf_op jit(solution)/shard_map/all_gather | solution.py:10
  71.2 7.4 %copy-start.2 = (f32[4,512,1024]{2,1,0:T(8,128)S(1)}, f32[4,512,1024]{2,1,0:T(8,128)}, u32[]{:S(2)}) copy-start(f32[4,512,1024]{2,1,0:T(8,128)} %get-tuple-element.206) | copy-start | bytes 25165828 | tf_op jit(solution)/shard_map/while
  88.0 7.4 %copy-start.2 = (f32[4,512,1024]{2,1,0:T(8,128)S(1)}, f32[4,512,1024]{2,1,0:T(8,128)}, u32[]{:S(2)}) copy-start(f32[4,512,1024]{2,1,0:T(8,128)} %get-tuple-element.206) | copy-start | bytes 25165828 | tf_op jit(solution)/shard_map/while
  104.7 7.4 %copy-start.2 = (f32[4,512,1024]{2,1,0:T(8,128)S(1)}, f32[4,512,1024]{2,1,0:T(8,128)}, u32[]{:S(2)}) copy-start(f32[4,512,1024]{2,1,0:T(8,128)} %get-tuple-element.206) | copy-start | bytes 25165828 | tf_op jit(solution)/shard_map/while
  121.4 7.4 %copy-start.2 = (f32[4,512,1024]{2,1,0:T(8,128)S(1)}, f32[4,512,1024]{2,1,0:T(8,128)}, u32[]{:S(2)}) copy-start(f32[4,512,1024]{2,1,0:T(8,128)} %get-tuple-element.206) | copy-start | bytes 25165828 | tf_op jit(solution)/shard_map/while
  138.2 7.4 %copy-start.2 = (f32[4,512,1024]{2,1,0:T(8,128)S(1)}, f32[4,512,1024]{2,1,0:T(8,128)}, u32[]{:S(2)}) copy-start(f32[4,512,1024]{2,1,0:T(8,128)} %get-tuple-element.206) | copy-start | bytes 25165828 | tf_op jit(solution)/shard_map/while
  154.9 7.4 %copy-start.2 = (f32[4,512,1024]{2,1,0:T(8,128)S(1)}, f32[4,512,1024]{2,1,0:T(8,128)}, u32[]{:S(2)}) copy-start(f32[4,512,1024]{2,1,0:T(8,128)} %get-tuple-element.206) | copy-start | bytes 25165828 | tf_op jit(solution)/shard_map/while
  163.8 1.3 copy-start.1
  165.0 1.5 copy-start.5
  165.0 2.1 copy-start.3
  165.0 6.4 %copy-start.4 = (s32[24]{0:T(128)S(1)}, s32[24]{0:T(128)}, u32[]{:S(2)}) copy-start(s32[24]{0:T(128)} %param.12) | copy-start | bytes 292
Sparse Core Ops, SparseCore 0:
  10.1 53.1 all-gather.2
  165.1 25.4 all-gather.4
where the time goes:
time: 270 us
  blocking collectives  113 us (42%)
  matrix products  77.7 us (29%)
  local copies, waits for them, and re-layouts  27.5 us (10%)
  waiting for transfers between devices  25.6 us (9%)
  between operations  14.3 us (5%)
  other arithmetic  11.1 us (4%)
    unnamed x1, blocking collectives  60.1 us
    dot_general x6, matrix products, attend(): jnp.einsum('gij,gdj->gdi', exponent, tile_geometry, precision=highest)  44.3 us
    dot_general x6, matrix products, attend(): jnp.einsum('gic,gjc->gij', queries, key_rows, preferred_element_type=jnp....  27.1 us
    all_gather x1, blocking collectives, per_device(): lax.all_gather(geometry, 'pair', axis=0, tiled=True)  23.6 us
    all_gather x1, waiting for transfers between devices, per_device(): lax.all_gather(descriptors, 'pair', axis=0, tiled=True)  21.4 us
    gather x6, local copies, waits for them, and re-layouts, attend(): key_rows = target_desc[tile_ids]  16.8 us
    all_gather x2, blocking collectives, merged(): everything = jax.tree.map(lambda part: lax.all_gather(part, axis), shard)  15.5 us
    all_gather x1, blocking collectives, per_device(): lax.all_gather(descriptors, 'split', axis=1, tiled=True)  9.42 us
  transfers between devices with their start and end apart: 2, of which 2 were waited for; matrix products, arithmetic and copies ran while one was open for 1% of the time, Pallas kernels for 0%

commit v1 on v0

v1 whole, which is shorter than its diff:
```python
import functools
import math

import jax
import jax.numpy as jnp
from jax import lax
from jax.experimental import pallas as pl
from jax.experimental.pallas import tpu as pltpu
from jax.sharding import PartitionSpec as P

NT = (((1,), (1,)), ((), ()))
NN = (((1,), (0,)), ((), ()))
PAD = 16


def fused(dims, meta, own_ref, pc_ref, ph_ref, pg_ref, blocks, src, mine, theirs, feats, tgrams, vown, vrecv,
          ring_send, ring_recv, part_send, part_recv, src_send, src_recv, par_send, par_recv, pose_send, pose_recv):
    n_pair, n_split, hr, width, tasks = dims
    half_ring = n_pair // 2
    reach = half_ring // 2
    n_sub = 2 * n_split
    rows = n_sub * hr
    factor = math.log2(math.e) * width ** -0.5
    p = lax.axis_index("pair")
    sp = lax.axis_index("split")
    core = p % 2
    group = p // 2
    partner = p + 1 - 2 * core
    odd = group % 2
    spot = (1 - odd) * (group // 2) + odd * (half_ring - 1 - group // 2)

    def pair_at(where, which):
        where = (where + half_ring) % half_ring
        late = where // reach
        return ((1 - late) * 2 * where + late * (2 * (half_ring - 1 - where) + 1)) * 2 + which

    def remote(a, b, s, r, device):
        return pltpu.make_async_remote_copy(a, b, s, r, device_id=device, device_id_type=pl.DeviceIdType.MESH)

    barrier = pltpu.get_barrier_semaphore()
    for f in range(1, n_pair):
        pl.semaphore_signal(barrier, inc=1, device_id={"pair": (p + f) % n_pair}, device_id_type=pl.DeviceIdType.MESH)
    for f in range(1, n_split):
        pl.semaphore_signal(barrier, inc=1, device_id={"split": (sp + f) % n_split}, device_id_type=pl.DeviceIdType.MESH)
    pl.semaphore_wait(barrier, n_pair + n_split - 2)

    goal = [pair_at(spot + 1, core), pair_at(spot - 1, core)]
    started = []

    def slot_of(way, d, which):
        return pair_at(spot - d if way == 0 else spot + d, which)

    def ring_copy(way, d, h, source):
        slot = slot_of(way, d, core)
        a = own_ref.at[h] if source else blocks.at[slot, h]
        return remote(a, blocks.at[slot, h], ring_send.at[way, d, h], ring_recv.at[way, d, h], {"pair": goal[way]})

    def ring_arrival(way, d, h):
        slot = slot_of(way, d, core)
        return remote(blocks.at[slot, h], blocks.at[slot, h], ring_send.at[way, d - 1, h], ring_recv.at[way, d - 1, h],
                      {"pair": goal[way]})

    def part_copy(way, d, h, source=False):
        slot = slot_of(way, d, core)
        a = own_ref.at[h] if source else blocks.at[slot, h]
        return remote(a, blocks.at[slot, h], part_send.at[way, d, h], part_recv.at[way, d, h], {"pair": partner})

    def part_arrival(way, d, h):
        slot = slot_of(way, d, 1 - core)
        return remote(blocks.at[slot, h], blocks.at[slot, h], part_send.at[way, d, h], part_recv.at[way, d, h],
                      {"pair": partner})

    def go(copy):
        copy.start()
        started.append(copy)

    for f in range(1, n_split):
        go(remote(own_ref, src.at[sp], src_send.at[f - 1], src_recv.at[f - 1], {"split": (sp + f) % n_split}))
    for h in range(2):
        for way in range(2):
            go(ring_copy(way, 0, h, True))
        go(part_copy(0, 0, h, True))
    src[sp] = own_ref[...]
    feats[p] = jnp.zeros_like(feats[p])
    for f in range(1, n_split):
        frm = (sp + n_split - f) % n_split
        remote(own_ref, src.at[frm], src_send.at[f - 1], src_recv.at[f - 1], {"split": frm}).wait_recv()

    row8 = lax.broadcasted_iota(jnp.int32, (8, hr), 0)

    def attend(slot):
        for u in range(n_sub):
            queries = src[u // 2, u % 2, :hr, :]
            scores = [lax.dot_general(blocks[slot, h, :hr, :], queries, NT, preferred_element_type=jnp.float32)
                      for h in range(2)]
            top = jnp.maximum(jnp.max(scores[0], axis=0, keepdims=True), jnp.max(scores[1], axis=0, keepdims=True))
            moment = None
            for h in range(2):
                weight = jnp.exp2((scores[h] - top) * factor)
                coarse = weight.astype(jnp.bfloat16)
                fine = (weight - coarse.astype(jnp.float32)).astype(jnp.bfloat16)
                shape = blocks[slot, h, hr:hr + PAD, :hr]
                for piece in (coarse, fine):
                    term = lax.dot_general(shape, piece, NN, preferred_element_type=jnp.float32)
                    moment = term if moment is None else moment + term
            mine[slot, u] = jnp.where(row8 == 7, top, moment[:8])

    order = []

    def process(items):
        slots = [slot_of(*item) for item in items]
        if len(slots) == 1:
            attend(slots[0])
        else:
            def body(k, carry):
                attend((1 - k) * slots[0] + k * slots[1])
                return carry
            lax.fori_loop(0, 2, body, 0)
        for slot in slots:
            index = len(order)
            order.append(slot)
            for f in range(1, n_split):
                go(remote(mine.at[slot], theirs.at[f - 1, slot], par_send.at[index, f - 1], par_recv.at[index, f - 1],
                          {"split": (sp + f) % n_split}))

    def take_partner(d, ways=(0, 1), halves=(0, 1)):
        for way in ways:
            for h in halves:
                part_arrival(way, d, h).wait_recv()

    for d in range(1, reach):
        for h in range(2):
            for way in range(2):
                ring_arrival(way, d, h).wait_recv()
                if d + 1 < reach or way == h:
                    go(ring_copy(way, d, h, False))
                go(part_copy(way, d, h))
            if h == 1:
                process([(0, d, core), (1, d, core)])
            elif d == 1:
                take_partner(0, (0,))
                process([(0, 0, 1 - core)])
            else:
                take_partner(d - 1)
                process([(0, d - 1, 1 - core), (1, d - 1, 1 - core)])
    take_partner(reach - 1)
    process([(0, reach - 1, 1 - core), (1, reach - 1, 1 - core)])
    for way in range(2):
        ring_arrival(way, reach, way).wait_recv()
        go(part_copy(way, reach, way))
    process([(0, reach, core)])
    for way in range(2):
        part_arrival(way, reach, way).wait_recv()
    process([(0, reach, 1 - core)])

    for index, slot in enumerate(order):
        for f in range(1, n_split):
            remote(mine.at[slot], theirs.at[f - 1, slot], par_send.at[index, f - 1], par_recv.at[index, f - 1],
                   {"split": (sp + f) % n_split}).wait_recv()

    def featurize(k, carry):
        slot = (p + 1 + k) % n_pair
        for u in range(n_sub):
            parts = [mine[slot, u]] + [theirs[f, slot, u] for f in range(n_split - 1)]
            top = parts[0][7:8]
            for part in parts[1:]:
                top = jnp.maximum(top, part[7:8])
            total = None
            for part in parts:
                term = part * jnp.exp2((part[7:8] - top) * factor)
                total = term if total is None else total + term
            soft = total / total[6:7]
            y = src[u // 2, u % 2, hr:hr + PAD, :hr].astype(jnp.float32)
            yv = [y[c:c + 1] for c in range(3)]
            mv = [soft[c:c + 1] for c in range(3)]
            nv = [soft[c:c + 1] for c in range(3, 6)]

            def cross(a, b):
                return [a[1] * b[2] - a[2] * b[1], a[2] * b[0] - a[0] * b[2], a[0] * b[1] - a[1] * b[0]]

            residual = nv[0] * (yv[0] - mv[0]) + nv[1] * (yv[1] - mv[1]) + nv[2] * (yv[2] - mv[2])
            zero = jnp.zeros_like(residual)
            minus = [-v for v in cross(mv, nv)] + [-v for v in nv]
            f16 = jnp.concatenate(cross(yv, nv) + nv + [residual, zero] + minus + [residual, zero], axis=0)
            coarse = f16.astype(jnp.bfloat16)
            fine = (f16 - coarse.astype(jnp.float32)).astype(jnp.bfloat16)
            feats[slot, :, u * hr:(u + 1) * hr] = jnp.concatenate([coarse, fine], axis=0)
        return carry

    lax.fori_loop(0, n_pair - 1, featurize, 0)

    lanes = 8 * n_pair
    row_ids = lax.broadcasted_iota(jnp.int32, (32, rows), 1)
    source_sum = jnp.zeros((8, 16), jnp.float32)
    for k in range(tasks):
        f = feats[meta[k]]
        live = jnp.where(row_ids < meta[tasks + k], f, jnp.zeros_like(f))
        gram = lax.dot_general(live, f, NT, preferred_element_type=jnp.float32)
        gram = gram[:16] + gram[16:]
        gram = (gram[:, :16] + gram[:, 16:]) * (1.0 / rows)
        pc_ref[k] = gram[0:6, 8:14]
        source_sum = source_sum + gram[:8]
        tgrams[k * 8:(k + 1) * 8, :] = gram[8:]
    spread_row = lax.broadcasted_iota(jnp.int32, (16, lanes), 0)
    spread_lane = lax.broadcasted_iota(jnp.int32, (16, lanes), 1)
    highest = lax.Precision.HIGHEST
    spread_target = (spread_lane % 8 == spread_row - 8).astype(jnp.float32)
    spread_source = (spread_lane % 8 == spread_row).astype(jnp.float32)
    wide = lax.dot_general(tgrams[...], spread_target, NN, precision=highest, preferred_element_type=jnp.float32)
    lane_scan = lax.broadcasted_iota(jnp.int32, (8, lanes), 1) // 8
    total = jnp.where(
        lane_scan == p,
        lax.dot_general(source_sum, spread_source, NN, precision=highest, preferred_element_type=jnp.float32), 0.0)
    for k in range(tasks):
        total = total + jnp.where(lane_scan == meta[k], wide[k * 8:(k + 1) * 8], 0.0)
    vown[...] = total
    for f in range(1, n_pair):
        go(remote(vown, vrecv.at[f - 1], pose_send.at[f - 1], pose_recv.at[f - 1], {"pair": (p + f) % n_pair}))
    scan = 0
    for k in range(n_pair):
        scan = scan + k * (meta[2 * tasks + k] == p).astype(jnp.int32)
    for f in range(1, n_pair):
        remote(vown, vrecv.at[f - 1], pose_send.at[f - 1], pose_recv.at[f - 1], {"pair": (p + f) % n_pair}).wait_recv()
    for f in range(n_pair - 1):
        total = total + vrecv[f]
    total = jnp.where(lane_scan == scan, total, 0.0) * (1.0 / tasks)
    gather_row = lax.broadcasted_iota(jnp.int32, (8, lanes), 0)
    gather_lane = lax.broadcasted_iota(jnp.int32, (8, lanes), 1)
    pick = (gather_lane % 8 == gather_row).astype(jnp.float32)
    result = lax.dot_general(total, pick, NT, precision=highest, preferred_element_type=jnp.float32)
    ph_ref[0] = result[0:6, 0:6]
    pg_ref[...] = result[6:7, 0:6]
    for copy in started:
        copy.wait_send()


def per_device(n_pair, n_split, descriptors, points, normals, pair_list, intersection, pose_index):
    block_rows, width = descriptors.shape[1:]
    hr = block_rows // 2
    tasks = intersection.shape[0]
    p = lax.axis_index("pair")
    targets = lax.dynamic_slice_in_dim(pair_list[:, 1], p * tasks, tasks, 0)
    meta = jnp.concatenate([targets, intersection, pose_index])
    geometry = jnp.concatenate(
        [points[0], normals[0], jnp.ones((1, block_rows), points.dtype), jnp.zeros((PAD - 7, block_rows), points.dtype)], axis=0)
    geometry = geometry.reshape(PAD, 2, hr).transpose(1, 0, 2)
    geometry = jnp.pad(geometry, ((0, 0), (0, 0), (0, width - hr)))
    own = jnp.concatenate([descriptors[0].reshape(2, hr, width), geometry], axis=1)
    n_sub = 2 * n_split
    reach = n_pair // 4
    peers = max(n_split - 1, 1)
    dims = (n_pair, n_split, hr, width, tasks)
    dma = pltpu.SemaphoreType.DMA
    vmem = pl.BlockSpec(memory_space=pltpu.VMEM)
    return pl.pallas_call(
        functools.partial(fused, dims),
        out_shape=(
            jax.ShapeDtypeStruct((tasks, 6, 6), jnp.float32),
            jax.ShapeDtypeStruct((1, 6, 6), jnp.float32),
            jax.ShapeDtypeStruct((1, 6), jnp.float32),
        ),
        in_specs=[pl.BlockSpec(memory_space=pltpu.SMEM), vmem],
        out_specs=(vmem, vmem, vmem),
        scratch_shapes=[
            pltpu.VMEM((n_pair, 2, hr + PAD, width), jnp.bfloat16),
            pltpu.VMEM((n_split, 2, hr + PAD, width), jnp.bfloat16),
            pltpu.VMEM((n_pair, n_sub, 8, hr), jnp.float32),
            pltpu.VMEM((peers, n_pair, n_sub, 8, hr), jnp.float32),
            pltpu.VMEM((n_pair, 32, n_sub * hr), jnp.bfloat16),
            pltpu.VMEM((tasks * 8, 16), jnp.float32),
            pltpu.VMEM((8, 8 * n_pair), jnp.float32),
            pltpu.VMEM((n_pair - 1, 8, 8 * n_pair), jnp.float32),
            dma((2, reach, 2)), dma((2, reach, 2)),
            dma((2, reach + 1, 2)), dma((2, reach + 1, 2)),
            dma((peers,)), dma((peers,)),
            dma((n_pair - 1, peers)), dma((n_pair - 1, peers)),
            dma((n_pair - 1,)), dma((n_pair - 1,)),
        ],
        compiler_params=pltpu.CompilerParams(collective_id=0, has_side_effects=True),
    )(meta, own)


def solution(mesh):
    in_specs = (
        P("pair", "split", None),
        P("pair", None, "split"),
        P("pair", None, "split"),
        P(),
        P("pair"),
        P(),
    )
    out_specs = (P("pair", None, None), P("pair", None, None), P("pair", None))
    body = functools.partial(per_device, mesh.shape["pair"], mesh.shape["split"])
    return jax.shard_map(body, mesh=mesh, in_specs=in_specs, out_specs=out_specs, check_vma=False)
```

time: 270 us -> 54.6 us (0.20)
  blocking collectives: 113 us -> 0 us
  matrix products: 77.7 us -> 0 us
  Pallas kernels: 0 us -> 47.8 us
  waiting for transfers between devices: 25.6 us -> 0 us
  local copies, waits for them, and re-layouts: 27.5 us -> 3.55 us
  between operations: 14.3 us -> 0.68 us
  other arithmetic: 11.1 us -> 2.33 us
    dot_general x16 -> x0, matrix products: 77.7 us -> none  [the longest x6 44.3 us: attend(): jnp.einsum('gij,gdj->gdi', exponent, tile_geometry, precision=highest)]
    unnamed x1 -> x0, blocking collectives: 60.1 us -> none
    all_gather x5 -> x0, blocking collectives: 52.8 us -> none  [the longest x1 23.6 us: per_device(): lax.all_gather(geometry, 'pair', axis=0, tiled=True)]
    pallas_call x0 -> x1, Pallas kernels: none -> 47.8 us  [per_device(): pl.pallas_call(functools.partial(fused, dims), out_shape=(jax.ShapeDtypeS...]
    all_gather x2 -> x0, waiting for transfers between devices: 24.9 us -> none  [the longest x1 21.4 us: per_device(): lax.all_gather(descriptors, 'pair', axis=0, tiled=True)]
    gather x14 -> x0, local copies, waits for them, and re-layouts: 21.5 us -> none  [the longest x6 16.8 us: attend(): key_rows = target_desc[tile_ids]]
    reduce_sum x7 -> x0, other arithmetic: 8.46 us -> none  [the longest x6 8.41 us: attend(): totals = jnp.sum(exponent, axis=2)]
  transfers between devices with their start and end apart: 2 -> 0, of which waited for: 2 -> 0; matrix products, arithmetic and copies ran while one was open for 1% -> 0% of each run, Pallas kernels for 0% -> 0%
where the time goes in v1:
time: 54.6 us; the launch traced here: 54.3 us
  Pallas kernels  47.8 us (88%)
  local copies, waits for them, and re-layouts  3.55 us (7%)
  other arithmetic  2.33 us (4%)
  between operations  0.68 us (1%)
    pallas_call x1, Pallas kernels, per_device(): pl.pallas_call(functools.partial(fused, dims), out_shape=(jax.ShapeDtypeS...  47.8 us
    pallas_call x2, local copies, waits for them, and re-layouts, per_device(): pl.pallas_call(functools.partial(fused, dims), out_shape=(jax.ShapeDtypeS...  2.19 us
    concatenate x1, other arithmetic, per_device(): jnp.concatenate([descriptors[0].reshape(2, hr, width), geometry], axis=1)  1.67 us
    unnamed x15, local copies, waits for them, and re-layouts  1.13 us

profile of v1, /device:TPU:0, one launch (start us, length us, event | category | flops | bytes accessed | tf_op | source)
XLA Modules:
  0.0 54.3 jit_solution(14990850084318073434)
XLA Ops:
  0.6 0.0 copy-start.3
  0.6 0.1 pad.4.clone
  0.7 0.0 copy-start.4
  0.7 0.0 copy-start.5
  0.7 0.0 copy-start
  0.7 0.0 copy-start.1
  0.7 0.1 pad.5.clone
  0.8 0.5 copy-done.3
  1.3 0.1 dynamic-slice_bitcast_fusion
  1.4 0.0 copy-done.4
  1.4 0.0 copy-done.5
  1.4 0.6 %pad_add_fusion.meta = s32[64]{0:T(128)} fusion(s32[16]{0:T(128)S(1)} %copy-done.4, s32[24]{0:T(128)S(1)} %copy-done.5, s32[24]{0:T(128)S(1)} %dynamic-slice_bitcast_fusion), kind=kLoop, calls=%fused_computation.2 | loop fusion | flops 128 | bytes 512 | tf_op jit(solution)/shard_map/concatenate | solution.py:243
  2.0 0.0 copy-done
  2.0 0.0 copy-done.1
  2.0 0.1 maximum_bitcast_fusion
  2.1 1.7 %pad_maximum_fusion.own_ref = bf16[2,272,256]{2,1,0:T(8,128)(2,1)} fusion(bf16[2,16,256]{2,1,0:T(8,128)(2,1)S(1)} %maximum_bitcast_fusion, bf16[2,256,256]{2,1,0:T(8,128)(2,1)} %bitcast.8), kind=kLoop, calls=%fused_computation | loop fusion | flops 557056 | bytes 557056 | tf_op jit(solution)/shard_map/concatenate | solution.py:248
  3.7 47.8 %shard_map.85 = (f32[24,6,6]{2,1,0:T(8,128)}, f32[1,6,6]{2,1,0:T(8,128)}, f32[1,6]{1,0:T(1,128)}) custom-call(s32[64]{0:T(128)} %pad_add_fusion.meta, bf16[2,272,256]{2,1,0:T(8,128)(2,1)} %pad_maximum_fusion.own_ref), custom_call_target="tpu_custom_call" | custom-call | tf_op jit(solution)/shard_map/pallas_call | solution.py:255
  51.5 0.0 copy-start.2
  51.5 1.6 %copy.9 = f32[24,6,6]{0,2,1:T(8,128)} copy(f32[24,6,6]{2,1,0:T(8,128)} %get-tuple-element.3) | data formatting | bytes 6912 | tf_op jit(solution)/shard_map/pallas_call | solution.py:255
  53.1 0.0 copy-done.2
  53.1 0.0 copy-start.6
  53.1 0.6 %copy.10 = f32[1,6,6]{2,0,1:T(1,128)} copy(f32[1,6,6]{2,1,0:T(8,128)S(1)} %copy-done.2) | data formatting | bytes 288 | tf_op jit(solution)/shard_map/pallas_call | solution.py:255
  53.7 0.1 copy-done.6
  53.8 0.5 copy.12
  (2 shorter events, 0.0 us)
Async XLA Ops:
  0.6 0.7 %copy-start.3 = (s32[384,2]{0,1:T(2,128)S(1)}, s32[384,2]{0,1:T(2,128)}, u32[]{:S(2)}) copy-start(s32[384,2]{0,1:T(2,128)} %param.9) | copy-start | bytes 9220
  0.7 0.7 %copy-start.4 = (s32[16]{0:T(128)S(1)}, s32[16]{0:T(128)}, u32[]{:S(2)}) copy-start(s32[16]{0:T(128)} %param.11) | copy-start | bytes 196
  0.7 0.7 %copy-start.5 = (s32[24]{0:T(128)S(1)}, s32[24]{0:T(128)}, u32[]{:S(2)}) copy-start(s32[24]{0:T(128)} %param.10) | copy-start | bytes 292
  0.7 1.3 %copy-start = (bf16[1,3,512]{2,1,0:T(4,128)(2,1)S(1)}, bf16[1,3,512]{2,1,0:T(4,128)(2,1)}, u32[]{:S(2)}) copy-start(bf16[1,3,512]{2,1,0:T(4,128)(2,1)} %param.8) | copy-start | bytes 9220
  0.7 1.3 %copy-start.1 = (bf16[1,3,512]{2,1,0:T(4,128)(2,1)S(1)}, bf16[1,3,512]{2,1,0:T(4,128)(2,1)}, u32[]{:S(2)}) copy-start(bf16[1,3,512]{2,1,0:T(4,128)(2,1)} %param.7) | copy-start | bytes 9220
  51.5 1.6 %copy-start.2 = (f32[1,6,6]{2,1,0:T(8,128)S(1)}, f32[1,6,6]{2,1,0:T(8,128)}, u32[]{:S(2)}) copy-start(f32[1,6,6]{2,1,0:T(8,128)} %get-tuple-element.4) | copy-start | bytes 436
  53.1 0.7 %copy-start.6 = (f32[1,6]{1,0:T(1,128)S(1)}, f32[1,6]{1,0:T(1,128)}, u32[]{:S(2)}) copy-start(f32[1,6]{1,0:T(1,128)} %get-tuple-element.11) | copy-start | bytes 76

commit v2 on v1

v2 whole, which is shorter than its diff:
```python
import functools
import math

import jax
import jax.numpy as jnp
from jax import lax
from jax.experimental import pallas as pl
from jax.experimental.pallas import tpu as pltpu
from jax.sharding import PartitionSpec as P

NT = (((1,), (1,)), ((), ()))
NN = (((1,), (0,)), ((), ()))
PAD = 16
PIECES = 4


def fused(dims, meta, desc_ref, points_ref, normals_ref, pc_ref, ph_ref, pg_ref, own_ref, blocks, src, mine, theirs, feats, tgrams,
          vown, vrecv, ring_send, ring_recv, part_send, part_recv, src_send, src_recv, par_send, par_recv, pose_send, pose_recv):
    n_pair, n_split, hr, width, tasks = dims
    half_ring = n_pair // 2
    reach = half_ring // 2
    n_sub = 2 * n_split
    rows = n_sub * hr
    quarter = hr // 2
    cuts = [0] + [PAD + (q + 1) * quarter for q in range(PIECES)]
    factor = math.log2(math.e) * width ** -0.5
    p = lax.axis_index("pair")
    sp = lax.axis_index("split")
    core = p % 2
    group = p // 2
    partner = p + 1 - 2 * core
    odd = group % 2
    spot = (1 - odd) * (group // 2) + odd * (half_ring - 1 - group // 2)

    def pair_at(where, which):
        where = (where + half_ring) % half_ring
        late = where // reach
        return ((1 - late) * 2 * where + late * (2 * (half_ring - 1 - where) + 1)) * 2 + which

    def remote(a, b, s, r, device):
        return pltpu.make_async_remote_copy(a, b, s, r, device_id=device, device_id_type=pl.DeviceIdType.MESH)

    own_ref[PAD:, :] = desc_ref[0]
    geometry = jnp.concatenate(
        [points_ref[0].astype(jnp.float32), normals_ref[0].astype(jnp.float32), jnp.ones((1, 2 * hr), jnp.float32),
         jnp.zeros((1, 2 * hr), jnp.float32)], axis=0)
    geometry = jnp.concatenate([geometry[:, :hr], geometry[:, hr:]], axis=0).astype(jnp.bfloat16)
    if hr < width:
        own_ref[0:PAD, :] = jnp.zeros((PAD, width), jnp.bfloat16)
    own_ref[0:PAD, :hr] = geometry
    src[sp] = own_ref[...]
    feats[p] = jnp.zeros_like(feats[p])

    barrier = pltpu.get_barrier_semaphore()
    for f in range(1, n_pair):
        pl.semaphore_signal(barrier, inc=1, device_id={"pair": (p + f) % n_pair}, device_id_type=pl.DeviceIdType.MESH)
    for f in range(1, n_split):
        pl.semaphore_signal(barrier, inc=1, device_id={"split": (sp + f) % n_split}, device_id_type=pl.DeviceIdType.MESH)
    pl.semaphore_wait(barrier, n_pair + n_split - 2)

    goal = [pair_at(spot + 1, core), pair_at(spot - 1, core)]

    def slot_of(way, d, which):
        return pair_at(spot - d if way == 0 else spot + d, which)

    def piece(ref, q):
        return ref.at[pl.ds(cuts[q], cuts[q + 1] - cuts[q])]

    def ring_copy(way, d, q):
        slot = slot_of(way, d, core)
        source = own_ref if isinstance(d, int) and d == 0 else blocks.at[slot]
        return remote(piece(source, q), piece(blocks.at[slot], q), ring_send.at[way, d, q], ring_recv.at[way, d, q],
                      {"pair": goal[way]})

    def ring_arrival(way, d, q):
        here = piece(blocks.at[slot_of(way, d, core)], q)
        return remote(here, here, ring_send.at[way, d - 1, q], ring_recv.at[way, d - 1, q], {"pair": goal[way]})

    def part_copy(way, d, q):
        slot = slot_of(way, d, core)
        source = own_ref if isinstance(d, int) and d == 0 else blocks.at[slot]
        return remote(piece(source, q), piece(blocks.at[slot], q), part_send.at[way, d, q], part_recv.at[way, d, q],
                      {"pair": partner})

    def part_arrival(way, d, q):
        here = piece(blocks.at[slot_of(way, d, 1 - core)], q)
        return remote(here, here, part_send.at[way, d, q], part_recv.at[way, d, q], {"pair": partner})

    def src_copy(f, where):
        return remote(own_ref, src.at[where], src_send.at[f - 1], src_recv.at[f - 1], {"split": (sp + f) % n_split})

    def par_copy(index, slot, f):
        return remote(mine.at[slot], theirs.at[f - 1, slot], par_send.at[index, f - 1], par_recv.at[index, f - 1],
                      {"split": (sp + f) % n_split})

    for f in range(1, n_split):
        src_copy(f, sp).start()
    for q in range(PIECES):
        for way in range(2):
            ring_copy(way, 0, q).start()
        part_copy(0, 0, q).start()

    row8 = lax.broadcasted_iota(jnp.int32, (8, hr), 0)

    def attend(slot):
        for u in range(n_sub):
            queries = src[u // 2, pl.ds(PAD + (u % 2) * hr, hr), :]
            scores = [lax.dot_general(blocks[slot, pl.ds(PAD + h * hr, hr), :], queries, NT, preferred_element_type=jnp.float32)
                      for h in range(2)]
            top = jnp.maximum(jnp.max(scores[0], axis=0, keepdims=True), jnp.max(scores[1], axis=0, keepdims=True))
            shape = blocks[slot, 0:PAD, :hr]
            moment = None
            for h in range(2):
                weight = jnp.exp2((scores[h] - top) * factor)
                coarse = weight.astype(jnp.bfloat16)
                fine = (weight - coarse.astype(jnp.float32)).astype(jnp.bfloat16)
                for piece in (coarse, fine):
                    term = lax.dot_general(shape, piece, NN, preferred_element_type=jnp.float32)[8 * h:8 * h + 8]
                    moment = term if moment is None else moment + term
            mine[slot, u] = jnp.where(row8 == 7, top, moment)

    def featurize(index, slot):
        for f in range(1, n_split):
            par_copy(index, slot, f).wait_recv()
        for u in range(n_sub):
            parts = [mine[slot, u]] + [theirs[f, slot, u] for f in range(n_split - 1)]
            top = parts[0][7:8]
            for part in parts[1:]:
                top = jnp.maximum(top, part[7:8])
            total = None
            for part in parts:
                term = part * jnp.exp2((part[7:8] - top) * factor)
                total = term if total is None else total + term
            soft = total / total[6:7]
            y = src[u // 2, 0:PAD, :hr].astype(jnp.float32)[8 * (u % 2):8 * (u % 2) + 8]
            yv = [y[c:c + 1] for c in range(3)]
            mv = [soft[c:c + 1] for c in range(3)]
            nv = [soft[c:c + 1] for c in range(3, 6)]

            def cross(a, b):
                return [a[1] * b[2] - a[2] * b[1], a[2] * b[0] - a[0] * b[2], a[0] * b[1] - a[1] * b[0]]

            residual = nv[0] * (yv[0] - mv[0]) + nv[1] * (yv[1] - mv[1]) + nv[2] * (yv[2] - mv[2])
            zero = jnp.zeros_like(residual)
            minus = [-v for v in cross(mv, nv)] + [-v for v in nv]
            f16 = jnp.concatenate(cross(yv, nv) + nv + [residual, zero] + minus + [residual, zero], axis=0)
            coarse = f16.astype(jnp.bfloat16)
            fine = (f16 - coarse.astype(jnp.float32)).astype(jnp.bfloat16)
            feats[slot, :, u * hr:(u + 1) * hr] = jnp.concatenate([coarse, fine], axis=0)

    def slot_at(index):
        d = (index + 3) // 4
        j = (index + 3) % 4
        way = j % 2
        which = (1 - j // 2) * core + (j // 2) * (1 - core)
        return pair_at(spot - (1 - 2 * way) * d, which)

    def process(index, slot, lagged):
        attend(slot)
        for f in range(1, n_split):
            par_copy(index, slot, f).start()
        if lagged:
            featurize(index - 2, slot_at(index - 2))

    def take_partner(way, d):
        for q in range(PIECES):
            part_arrival(way, d, q).wait_recv()

    def event(d, q, last):
        for way in range(2):
            ring_arrival(way, d, q).wait_recv()
            if last:
                @pl.when(d + 1 < reach)
                def _():
                    ring_copy(way, d, q).start()
                if way == q // 2:
                    @pl.when(d + 1 == reach)
                    def _():
                        ring_copy(way, d, q).start()
            else:
                ring_copy(way, d, q).start()
            part_copy(way, d, q).start()

    for q in range(PIECES):
        event(1, q, reach == 2)
    for f in range(1, n_split):
        src_copy(f, (sp + n_split - f) % n_split).wait_recv()
    take_partner(0, 0)
    process(0, slot_at(0), False)
    process(1, slot_at(1), False)

    def stage(d, carry):
        base = 4 * d - 6
        for q in range(PIECES):
            event(d, q, True)
            if q in (1, 2):
                take_partner(q - 1, d - 1)
            process(base + q, slot_at(base + q), True)
        return carry

    lax.fori_loop(2, reach, stage, 0)
    base = 4 * reach - 6
    final_own = slot_of(0, reach, core)
    final_partner = slot_of(0, reach, 1 - core)
    half_pieces = PIECES // 2
    for k in range(half_pieces):
        for way in range(2):
            q = way * half_pieces + k
            ring_arrival(way, reach, q).wait_recv()
            part_copy(way, reach, q).start()
        if k == 0:
            process(base, slot_at(base), True)
            take_partner(0, reach - 1)
            process(base + 1, slot_at(base + 1), True)
    take_partner(1, reach - 1)
    process(base + 2, slot_at(base + 2), True)
    process(base + 3, final_own, True)
    for way in range(2):
        for k in range(half_pieces):
            part_arrival(way, reach, way * half_pieces + k).wait_recv()
    process(base + 4, final_partner, True)
    featurize(base + 3, final_own)
    featurize(base + 4, final_partner)

    lanes = 8 * n_pair
    row_ids = lax.broadcasted_iota(jnp.int32, (32, rows), 1)
    source_sum = jnp.zeros((8, 16), jnp.float32)
    for k in range(tasks):
        f = feats[meta[k]]
        live = jnp.where(row_ids < meta[tasks + k], f, jnp.zeros_like(f))
        gram = lax.dot_general(live, f, NT, preferred_element_type=jnp.float32)
        gram = gram[:16] + gram[16:]
        gram = (gram[:, :16] + gram[:, 16:]) * (1.0 / rows)
        pc_ref[k] = gram[0:6, 8:14]
        source_sum = source_sum + gram[:8]
        tgrams[k * 8:(k + 1) * 8, :] = gram[8:]
    spread_row = lax.broadcasted_iota(jnp.int32, (16, lanes), 0)
    spread_lane = lax.broadcasted_iota(jnp.int32, (16, lanes), 1)
    highest = lax.Precision.HIGHEST
    spread_target = (spread_lane % 8 == spread_row - 8).astype(jnp.float32)
    spread_source = (spread_lane % 8 == spread_row).astype(jnp.float32)
    wide = lax.dot_general(tgrams[...], spread_target, NN, precision=highest, preferred_element_type=jnp.float32)
    lane_scan = lax.broadcasted_iota(jnp.int32, (8, lanes), 1) // 8
    total = jnp.where(
        lane_scan == p,
        lax.dot_general(source_sum, spread_source, NN, precision=highest, preferred_element_type=jnp.float32), 0.0)
    for k in range(tasks):
        total = total + jnp.where(lane_scan == meta[k], wide[k * 8:(k + 1) * 8], 0.0)
    vown[...] = total
    for f in range(1, n_pair):
        remote(vown, vrecv.at[f - 1], pose_send.at[f - 1], pose_recv.at[f - 1], {"pair": (p + f) % n_pair}).start()
    scan = 0
    for k in range(n_pair):
        scan = scan + k * (meta[2 * tasks + k] == p).astype(jnp.int32)
    for f in range(1, n_pair):
        remote(vown, vrecv.at[f - 1], pose_send.at[f - 1], pose_recv.at[f - 1], {"pair": (p + f) % n_pair}).wait_recv()
    for f in range(n_pair - 1):
        total = total + vrecv[f]
    total = jnp.where(lane_scan == scan, total, 0.0) * (1.0 / tasks)
    gather_row = lax.broadcasted_iota(jnp.int32, (8, lanes), 0)
    gather_lane = lax.broadcasted_iota(jnp.int32, (8, lanes), 1)
    pick = (gather_lane % 8 == gather_row).astype(jnp.float32)
    result = lax.dot_general(total, pick, NT, precision=highest, preferred_element_type=jnp.float32)
    ph_ref[0] = result[0:6, 0:6]
    pg_ref[...] = result[6:7, 0:6]
    for f in range(1, n_pair):
        remote(vown, vrecv.at[f - 1], pose_send.at[f - 1], pose_recv.at[f - 1], {"pair": (p + f) % n_pair}).wait_send()
    for f in range(1, n_split):
        src_copy(f, sp).wait_send()

        def sent(index, carry):
            par_copy(index, slot_at(index), f).wait_send()
            return carry

        lax.fori_loop(0, n_pair - 2, sent, 0)
        par_copy(n_pair - 2, final_partner, f).wait_send()
    for q in range(PIECES):
        part_copy(0, 0, q).wait_send()
        for way in range(2):
            ring_copy(way, 0, q).wait_send()
            if way == q // half_pieces:
                ring_copy(way, reach - 1, q).wait_send()
                part_copy(way, reach, q).wait_send()

    def drained(d, carry):
        for q in range(PIECES):
            for way in range(2):
                part_copy(way, d, q).wait_send()

                @pl.when(d + 1 < reach)
                def _():
                    ring_copy(way, d, q).wait_send()
        return carry

    lax.fori_loop(1, reach, drained, 0)


def per_device(n_pair, n_split, descriptors, points, normals, pair_list, intersection, pose_index):
    block_rows, width = descriptors.shape[1:]
    hr = block_rows // 2
    tasks = intersection.shape[0]
    p = lax.axis_index("pair")
    targets = lax.dynamic_slice_in_dim(pair_list[:, 1], p * tasks, tasks, 0)
    meta = jnp.concatenate([targets, intersection, pose_index])
    n_sub = 2 * n_split
    reach = n_pair // 4
    peers = max(n_split - 1, 1)
    dims = (n_pair, n_split, hr, width, tasks)
    dma = pltpu.SemaphoreType.DMA
    vmem = pl.BlockSpec(memory_space=pltpu.VMEM)
    return pl.pallas_call(
        functools.partial(fused, dims),
        out_shape=(
            jax.ShapeDtypeStruct((tasks, 6, 6), jnp.float32),
            jax.ShapeDtypeStruct((1, 6, 6), jnp.float32),
            jax.ShapeDtypeStruct((1, 6), jnp.float32),
        ),
        in_specs=[pl.BlockSpec(memory_space=pltpu.SMEM), vmem, vmem, vmem],
        out_specs=(vmem, vmem, vmem),
        scratch_shapes=[
            pltpu.VMEM((block_rows + PAD, width), jnp.bfloat16),
            pltpu.VMEM((n_pair, block_rows + PAD, width), jnp.bfloat16),
            pltpu.VMEM((n_split, block_rows + PAD, width), jnp.bfloat16),
            pltpu.VMEM((n_pair, n_sub, 8, hr), jnp.float32),
            pltpu.VMEM((peers, n_pair, n_sub, 8, hr), jnp.float32),
            pltpu.VMEM((n_pair, 32, n_sub * hr), jnp.bfloat16),
            pltpu.VMEM((tasks * 8, 16), jnp.float32),
            pltpu.VMEM((8, 8 * n_pair), jnp.float32),
            pltpu.VMEM((n_pair - 1, 8, 8 * n_pair), jnp.float32),
            dma((2, reach, PIECES)), dma((2, reach, PIECES)),
            dma((2, reach + 1, PIECES)), dma((2, reach + 1, PIECES)),
            dma((peers,)), dma((peers,)),
            dma((n_pair - 1, peers)), dma((n_pair - 1, peers)),
            dma((n_pair - 1,)), dma((n_pair - 1,)),
        ],
        compiler_params=pltpu.CompilerParams(collective_id=0, has_side_effects=True),
    )(meta, descriptors, points, normals)


def solution(mesh):
    in_specs = (
        P("pair", "split", None),
        P("pair", None, "split"),
        P("pair", None, "split"),
        P(),
        P("pair"),
        P(),
    )
    out_specs = (P("pair", None, None), P("pair", None, None), P("pair", None))
    body = functools.partial(per_device, mesh.shape["pair"], mesh.shape["split"])
    return jax.shard_map(body, mesh=mesh, in_specs=in_specs, out_specs=out_specs, check_vma=False)
```

time: 54.6 us -> 60.6 us (1.11)
  Pallas kernels: 47.8 us -> 55 us
  other arithmetic: 2.33 us -> 0.59 us
    pallas_call x1, Pallas kernels: 47.8 us -> 55 us  [per_device(): pl.pallas_call(functools.partial(fused, dims), out_shape=(jax.ShapeDtypeS...]
    concatenate x1 -> x0, other arithmetic: 1.67 us -> none  [per_device(): jnp.concatenate([descriptors[0].reshape(2, hr, width), geometry], axis=1)]
    unnamed x15 -> x11, local copies, waits for them, and re-layouts: 1.13 us -> 1.82 us
where the time goes in v2:
time: 60.6 us; the launch traced here: 60.3 us
  Pallas kernels  55 us (91%)
  local copies, waits for them, and re-layouts  4.09 us (7%)
  between operations  0.67 us (1%)
    pallas_call x1, Pallas kernels, per_device(): pl.pallas_call(functools.partial(fused, dims), out_shape=(jax.ShapeDtypeS...  55 us
    pallas_call x2, local copies, waits for them, and re-layouts, per_device(): pl.pallas_call(functools.partial(fused, dims), out_shape=(jax.ShapeDtypeS...  2.19 us
    unnamed x11, local copies, waits for them, and re-layouts  1.82 us

profile of v2, /device:TPU:0, one launch (start us, length us, event | category | flops | bytes accessed | tf_op | source)
XLA Modules:
  0.0 60.3 jit_solution(7374012066274108983)
XLA Ops:
  0.6 0.0 copy-start.1
  0.6 0.7 %copy-done.1 = s32[384,2]{0,1:T(2,128)S(1)} copy-done((s32[384,2]{0,1:T(2,128)S(1)}, s32[384,2]{0,1:T(2,128)}, u32[]{:S(2)}) %copy-start.1) | copy-done | bytes 3096
  1.3 0.0 copy-start.2
  1.3 0.0 copy-start.3
  1.3 0.1 dynamic-slice_bitcast_fusion
  1.4 0.6 copy-done.2
  2.0 0.0 copy-done.3
  2.0 0.6 pad_add_fusion.meta
  2.6 55.0 %shard_map.85 = (f32[24,6,6]{2,1,0:T(8,128)}, f32[1,6,6]{2,1,0:T(8,128)}, f32[1,6]{1,0:T(1,128)}) custom-call(s32[64]{0:T(128)} %pad_add_fusion.meta, bf16[1,512,256]{2,1,0:T(8,128)(2,1)} %desc_ref.1, bf16[1,3,512]{2,1,0:T(4,128)(2,1)} %points_ref.1, bf16[1,3,512]{2,1,0:T(4,128)(2,1)} %normals_ref.1), custom_call_target="tpu_custom_call" | custom-call | tf_op jit(solution)/shard_map/pallas_call | solution.py:311
  57.6 0.0 copy-start
  57.6 1.6 %copy.9 = f32[24,6,6]{0,2,1:T(8,128)} copy(f32[24,6,6]{2,1,0:T(8,128)} %get-tuple-element.3) | data formatting | bytes 6912 | tf_op jit(solution)/shard_map/pallas_call | solution.py:311
  59.2 0.0 copy-done
  59.2 0.0 copy-start.4
  59.2 0.6 copy.10
  59.8 0.0 copy-done.4
  59.8 0.5 copy.12
  (1 shorter events, 0.0 us)
Async XLA Ops:
  0.6 0.7 %copy-start.1 = (s32[384,2]{0,1:T(2,128)S(1)}, s32[384,2]{0,1:T(2,128)}, u32[]{:S(2)}) copy-start(s32[384,2]{0,1:T(2,128)} %param.9) | copy-start | bytes 9220
  1.3 0.7 %copy-start.2 = (s32[16]{0:T(128)S(1)}, s32[16]{0:T(128)}, u32[]{:S(2)}) copy-start(s32[16]{0:T(128)} %param.11) | copy-start | bytes 196
  1.3 0.7 %copy-start.3 = (s32[24]{0:T(128)S(1)}, s32[24]{0:T(128)}, u32[]{:S(2)}) copy-start(s32[24]{0:T(128)} %param.10) | copy-start | bytes 292
  57.6 1.6 %copy-start = (f32[1,6,6]{2,1,0:T(8,128)S(1)}, f32[1,6,6]{2,1,0:T(8,128)}, u32[]{:S(2)}) copy-start(f32[1,6,6]{2,1,0:T(8,128)} %get-tuple-element.4) | copy-start | bytes 436
  59.2 0.6 %copy-start.4 = (f32[1,6]{1,0:T(1,128)S(1)}, f32[1,6]{1,0:T(1,128)}, u32[]{:S(2)}) copy-start(f32[1,6]{1,0:T(1,128)} %get-tuple-element.11) | copy-start | bytes 76

commit v3 on v2

--- a/solution.py
+++ b/solution.py
@@ -22,7 +22,7 @@
     n_sub = 2 * n_split
     rows = n_sub * hr
     quarter = hr // 2
-    cuts = [0] + [PAD + (q + 1) * quarter for q in range(PIECES)]
+    cuts = [0] + [2 * PAD + (q + 1) * quarter for q in range(PIECES)]
     factor = math.log2(math.e) * width ** -0.5
     p = lax.axis_index("pair")
     sp = lax.axis_index("split")
@@ -40,14 +40,14 @@
     def remote(a, b, s, r, device):
         return pltpu.make_async_remote_copy(a, b, s, r, device_id=device, device_id_type=pl.DeviceIdType.MESH)
 
-    own_ref[PAD:, :] = desc_ref[0]
+    own_ref[2 * PAD:, :] = desc_ref[0]
     geometry = jnp.concatenate(
         [points_ref[0].astype(jnp.float32), normals_ref[0].astype(jnp.float32), jnp.ones((1, 2 * hr), jnp.float32),
-         jnp.zeros((1, 2 * hr), jnp.float32)], axis=0)
+         jnp.zeros((PAD - 7, 2 * hr), jnp.float32)], axis=0)
     geometry = jnp.concatenate([geometry[:, :hr], geometry[:, hr:]], axis=0).astype(jnp.bfloat16)
     if hr < width:
-        own_ref[0:PAD, :] = jnp.zeros((PAD, width), jnp.bfloat16)
-    own_ref[0:PAD, :hr] = geometry
+        own_ref[0:2 * PAD, :] = jnp.zeros((2 * PAD, width), jnp.bfloat16)
+    own_ref[0:2 * PAD, :hr] = geometry
     src[sp] = own_ref[...]
     feats[p] = jnp.zeros_like(feats[p])
 
@@ -104,20 +104,20 @@
 
     def attend(slot):
         for u in range(n_sub):
-            queries = src[u // 2, pl.ds(PAD + (u % 2) * hr, hr), :]
-            scores = [lax.dot_general(blocks[slot, pl.ds(PAD + h * hr, hr), :], queries, NT, preferred_element_type=jnp.float32)
+            queries = src[u // 2, pl.ds(2 * PAD + (u % 2) * hr, hr), :]
+            scores = [lax.dot_general(blocks[slot, pl.ds(2 * PAD + h * hr, hr), :], queries, NT, preferred_element_type=jnp.float32)
                       for h in range(2)]
             top = jnp.maximum(jnp.max(scores[0], axis=0, keepdims=True), jnp.max(scores[1], axis=0, keepdims=True))
-            shape = blocks[slot, 0:PAD, :hr]
             moment = None
             for h in range(2):
+                shape = blocks[slot, h * PAD:(h + 1) * PAD, :hr]
                 weight = jnp.exp2((scores[h] - top) * factor)
                 coarse = weight.astype(jnp.bfloat16)
                 fine = (weight - coarse.astype(jnp.float32)).astype(jnp.bfloat16)
                 for piece in (coarse, fine):
-                    term = lax.dot_general(shape, piece, NN, preferred_element_type=jnp.float32)[8 * h:8 * h + 8]
+                    term = lax.dot_general(shape, piece, NN, preferred_element_type=jnp.float32)
                     moment = term if moment is None else moment + term
-            mine[slot, u] = jnp.where(row8 == 7, top, moment)
+            mine[slot, u] = jnp.where(row8 == 7, top, moment[:8])
 
     def featurize(index, slot):
         for f in range(1, n_split):
@@ -132,7 +132,7 @@
                 term = part * jnp.exp2((part[7:8] - top) * factor)
                 total = term if total is None else total + term
             soft = total / total[6:7]
-            y = src[u // 2, 0:PAD, :hr].astype(jnp.float32)[8 * (u % 2):8 * (u % 2) + 8]
+            y = src[u // 2, (u % 2) * PAD:(u % 2) * PAD + PAD, :hr].astype(jnp.float32)
             yv = [y[c:c + 1] for c in range(3)]
             mv = [soft[c:c + 1] for c in range(3)]
             nv = [soft[c:c + 1] for c in range(3, 6)]
@@ -159,8 +159,6 @@
         attend(slot)
         for f in range(1, n_split):
             par_copy(index, slot, f).start()
-        if lagged:
-            featurize(index - 2, slot_at(index - 2))
 
     def take_partner(way, d):
         for q in range(PIECES):
@@ -219,7 +217,11 @@
         for k in range(half_pieces):
             part_arrival(way, reach, way * half_pieces + k).wait_recv()
     process(base + 4, final_partner, True)
-    featurize(base + 3, final_own)
+    def features(index, carry):
+        featurize(index, slot_at(index))
+        return carry
+
+    lax.fori_loop(0, n_pair - 2, features, 0)
     featurize(base + 4, final_partner)
 
     lanes = 8 * n_pair
@@ -318,9 +320,9 @@
         in_specs=[pl.BlockSpec(memory_space=pltpu.SMEM), vmem, vmem, vmem],
         out_specs=(vmem, vmem, vmem),
         scratch_shapes=[
-            pltpu.VMEM((block_rows + PAD, width), jnp.bfloat16),
-            pltpu.VMEM((n_pair, block_rows + PAD, width), jnp.bfloat16),
-            pltpu.VMEM((n_split, block_rows + PAD, width), jnp.bfloat16),
+            pltpu.VMEM((block_rows + 2 * PAD, width), jnp.bfloat16),
+            pltpu.VMEM((n_pair, block_rows + 2 * PAD, width), jnp.bfloat16),
+            pltpu.VMEM((n_split, block_rows + 2 * PAD, width), jnp.bfloat16),
             pltpu.VMEM((n_pair, n_sub, 8, hr), jnp.float32),
             pltpu.VMEM((peers, n_pair, n_sub, 8, hr), jnp.float32),
             pltpu.VMEM((n_pair, 32, n_sub * hr), jnp.bfloat16),

time: 60.6 us -> 52.6 us (0.87)
  Pallas kernels: 55 us -> 47.1 us
    pallas_call x1, Pallas kernels: 55 us -> 47.1 us  [per_device(): pl.pallas_call(functools.partial(fused, dims), out_shape=(jax.ShapeDtypeS...]
where the time goes in v3:
time: 52.6 us; the launch traced here: 52.4 us
  Pallas kernels  47.1 us (90%)
  local copies, waits for them, and re-layouts  4.09 us (8%)
  between operations  0.67 us (1%)
  other arithmetic  0.59 us (1%)
    pallas_call x1, Pallas kernels, per_device(): pl.pallas_call(functools.partial(fused, dims), out_shape=(jax.ShapeDtypeS...  47.1 us
    pallas_call x2, local copies, waits for them, and re-layouts, per_device(): pl.pallas_call(functools.partial(fused, dims), out_shape=(jax.ShapeDtypeS...  2.19 us
    unnamed x11, local copies, waits for them, and re-layouts  1.82 us

profile of v3, /device:TPU:0, one launch (start us, length us, event | category | flops | bytes accessed | tf_op | source)
XLA Modules:
  0.0 52.4 jit_solution(12918258270480171547)
XLA Ops:
  0.6 0.0 copy-start.1
  0.6 0.7 %copy-done.1 = s32[384,2]{0,1:T(2,128)S(1)} copy-done((s32[384,2]{0,1:T(2,128)S(1)}, s32[384,2]{0,1:T(2,128)}, u32[]{:S(2)}) %copy-start.1) | copy-done | bytes 3096
  1.3 0.0 copy-start.2
  1.3 0.0 copy-start.3
  1.3 0.1 dynamic-slice_bitcast_fusion
  1.4 0.6 %copy-done.2 = s32[16]{0:T(128)S(1)} copy-done((s32[16]{0:T(128)S(1)}, s32[16]{0:T(128)}, u32[]{:S(2)}) %copy-start.2) | copy-done | bytes 88
  2.0 0.0 copy-done.3
  2.0 0.6 %pad_add_fusion.meta = s32[64]{0:T(128)} fusion(s32[16]{0:T(128)S(1)} %copy-done.2, s32[24]{0:T(128)S(1)} %copy-done.3, s32[24]{0:T(128)S(1)} %dynamic-slice_bitcast_fusion), kind=kLoop, calls=%fused_computation | loop fusion | flops 128 | bytes 512 | tf_op jit(solution)/shard_map/concatenate | solution.py:306
  2.6 47.1 %shard_map.85 = (f32[24,6,6]{2,1,0:T(8,128)}, f32[1,6,6]{2,1,0:T(8,128)}, f32[1,6]{1,0:T(1,128)}) custom-call(s32[64]{0:T(128)} %pad_add_fusion.meta, bf16[1,512,256]{2,1,0:T(8,128)(2,1)} %desc_ref.1, bf16[1,3,512]{2,1,0:T(4,128)(2,1)} %points_ref.1, bf16[1,3,512]{2,1,0:T(4,128)(2,1)} %normals_ref.1), custom_call_target="tpu_custom_call" | custom-call | tf_op jit(solution)/shard_map/pallas_call | solution.py:313
  49.7 0.0 copy-start
  49.7 1.6 %copy.9 = f32[24,6,6]{0,2,1:T(8,128)} copy(f32[24,6,6]{2,1,0:T(8,128)} %get-tuple-element.3) | data formatting | bytes 6912 | tf_op jit(solution)/shard_map/pallas_call | solution.py:313
  51.3 0.0 copy-done
  51.3 0.0 copy-start.4
  51.3 0.6 %copy.10 = f32[1,6,6]{2,0,1:T(1,128)} copy(f32[1,6,6]{2,1,0:T(8,128)S(1)} %copy-done) | data formatting | bytes 288 | tf_op jit(solution)/shard_map/pallas_call | solution.py:313
  51.9 0.0 copy-done.4
  51.9 0.5 copy.12
  (1 shorter events, 0.0 us)
Async XLA Ops:
  0.6 0.7 %copy-start.1 = (s32[384,2]{0,1:T(2,128)S(1)}, s32[384,2]{0,1:T(2,128)}, u32[]{:S(2)}) copy-start(s32[384,2]{0,1:T(2,128)} %param.9) | copy-start | bytes 9220
  1.3 0.7 %copy-start.2 = (s32[16]{0:T(128)S(1)}, s32[16]{0:T(128)}, u32[]{:S(2)}) copy-start(s32[16]{0:T(128)} %param.11) | copy-start | bytes 196
  1.3 0.7 %copy-start.3 = (s32[24]{0:T(128)S(1)}, s32[24]{0:T(128)}, u32[]{:S(2)}) copy-start(s32[24]{0:T(128)} %param.10) | copy-start | bytes 292
  49.7 1.6 %copy-start = (f32[1,6,6]{2,1,0:T(8,128)S(1)}, f32[1,6,6]{2,1,0:T(8,128)}, u32[]{:S(2)}) copy-start(f32[1,6,6]{2,1,0:T(8,128)} %get-tuple-element.4) | copy-start | bytes 436
  51.3 0.6 %copy-start.4 = (f32[1,6]{1,0:T(1,128)S(1)}, f32[1,6]{1,0:T(1,128)}, u32[]{:S(2)}) copy-start(f32[1,6]{1,0:T(1,128)} %get-tuple-element.11) | copy-start | bytes 76
